TPU v7x, 256 devices: a whole 4x4x8 slice. The times are simulated.
256 devices in a mesh: dp: 16 (over y, z_hi), expert: 8 (over x, core), tensor: 2 (over z_lo).
Axes of the slice: x: 4, y: 4, z: 8 (z_hi: 4, z_lo: 2; z = z_hi * 2 + z_lo), core: 2. Of those that a mesh axis runs over, the one named last changes fastest.
Arguments:
- tokens: bfloat16 [2048, 5120], P('dp', 'tensor'), may hold values from -6 to 6
- routes: int32 [2048, 6], P('dp'), may hold values from 0 to 15, all different within a row; in each aligned block of 128 rows (0 to 127, 128 to 255, ...) at most 72 rows name the same one
- route_weights: float32 [2048, 6], P('dp'), may hold values from 0.05 to 0.5
- gate_weight: bfloat16 [16, 1536, 5120], P('dp', 'expert', 'tensor'), may hold values from -0.078125 to 0.078125
- up_weight: bfloat16 [16, 1536, 5120], P('dp', 'expert', 'tensor'), may hold values from -0.078125 to 0.078125
- down_weight: bfloat16 [16, 1536, 5120], P('dp', 'expert', 'tensor'), may hold values from -0.15625 to 0.15625
- cotangent: bfloat16 [2048, 5120], P('dp', 'tensor'), may hold values from -6 to 6
Outputs:
- layer_out: bfloat16 [2048, 5120], P('dp', 'tensor')
- token_grad: bfloat16 [2048, 5120], P('dp', 'tensor')
- gate_grad: float32 [16, 1536, 5120], P('dp', 'expert', 'tensor')
- up_grad: float32 [16, 1536, 5120], P('dp', 'expert', 'tensor')
- down_grad: float32 [16, 1536, 5120], P('dp', 'expert', 'tensor')
Inputs may be any that keep to these rules, and one draw needn't show every extreme that they name: `routes`: each row names 6 different experts. In the rows of one index of dp (aligned blocks of 128 rows) no expert is named by more than 72 rows, a bound that some block reaches.
All inputs are finite; a program needn't handle non-finite values.
Results may differ from a plain program's by a relative error of at most 0.023.
Values may be sent and summed in bfloat16 or wider, within the bound.
A program may use at most 128 MiB of HBM per device.

v0:
```python
import jax
import jax.numpy as jnp
from jax import lax
from jax.sharding import PartitionSpec as P


def body(tokens, routes, route_weights, gate_weight, up_weight, down_weight, cotangent):
    dp_count = lax.axis_size("dp")
    hidden_split = lax.axis_size("expert")
    gate_weight, up_weight, down_weight = (gate_weight[0], up_weight[0], down_weight[0])
    hidden_share, half_width = gate_weight.shape
    tok_rows, top_count = routes.shape
    experts = dp_count
    capacity = min(tok_rows, 3 * tok_rows * top_count // (2 * experts))
    share_rows = capacity // hidden_split
    own_rows = experts * share_rows
    pair_count = tok_rows * top_count
    flat_route = routes.T.reshape(pair_count)
    onehot = flat_route[:, None] == jnp.arange(experts, dtype=jnp.int32)[None, :]
    running = jnp.cumsum(onehot.astype(jnp.int32), axis=0) - 1
    position = jnp.sum(jnp.where(onehot, running, 0), axis=1)
    target = flat_route * capacity + position
    member = lax.axis_index("expert")
    own_index = jnp.arange(own_rows, dtype=jnp.int32)
    own_slot = own_index // share_rows * capacity + member * share_rows + own_index % share_rows
    selector = (own_slot[:, None] == target[None, :]).reshape(own_rows, top_count, tok_rows)
    weight_grid = jnp.sum(jnp.where(selector, route_weights.T[None], jnp.float32(0.0)), axis=1)
    own_weight = jnp.sum(weight_grid, axis=1, keepdims=True)
    own_place = jnp.any(selector, axis=1).astype(jnp.bfloat16)

    def select(values):
        return jnp.dot(own_place, values, preferred_element_type=jnp.float32)

    def dispatch(rows):
        arrived = lax.all_to_all(
            rows.reshape(dp_count, share_rows, half_width),
            "dp",
            split_axis=0,
            concat_axis=0,
            tiled=True,
        )
        return lax.all_gather(arrived.reshape(own_rows, half_width), "expert", axis=0, tiled=True)

    def width_sum(partial_values):
        mine = partial_values.astype(jnp.bfloat16)
        other = lax.ppermute(mine, "tensor", [(0, 1), (1, 0)])
        return mine.astype(jnp.float32) + other.astype(jnp.float32)

    def home(partial_rows):
        summed = lax.psum_scatter(
            partial_rows.astype(jnp.bfloat16), "expert", scatter_dimension=0, tiled=True
        )
        returned = lax.all_to_all(
            summed.reshape(dp_count, share_rows, half_width),
            "dp",
            split_axis=0,
            concat_axis=0,
            tiled=True,
        )
        return returned.reshape(own_rows, half_width)

    def token_sum(partial_tokens):
        part = lax.psum_scatter(
            partial_tokens.astype(jnp.bfloat16), "expert", scatter_dimension=0, tiled=True
        )
        return lax.all_gather(part, "expert", axis=0, tiled=True)

    rows = dispatch(select(tokens).astype(jnp.bfloat16))
    grad_rows = dispatch((select(cotangent) * own_weight).astype(jnp.bfloat16))
    nt = (((1,), (1,)), ((), ()))
    nn = (((1,), (0,)), ((), ()))
    tn = (((0,), (0,)), ((), ()))

    def mm(a, b, dims):
        return lax.dot_general(a, b, dims, preferred_element_type=jnp.float32)

    gate_val = width_sum(mm(rows, gate_weight, nt))
    up_val = width_sum(mm(rows, up_weight, nt))
    sigmoid_gate = jax.nn.sigmoid(gate_val)
    activated = gate_val * sigmoid_gate
    hidden = (activated * up_val).astype(jnp.bfloat16)
    expert_out = home(mm(hidden, down_weight, nn))
    out_part = mm(weight_grid.astype(jnp.bfloat16), expert_out, tn)
    layer_out = token_sum(out_part)
    hidden_grad = width_sum(mm(grad_rows, down_weight, nt))
    gate_delta = (
        hidden_grad * up_val * sigmoid_gate * (1.0 + gate_val * (1.0 - sigmoid_gate))
    ).astype(jnp.bfloat16)
    up_delta = (hidden_grad * activated).astype(jnp.bfloat16)
    input_part = mm(gate_delta, gate_weight, nn) + mm(up_delta, up_weight, nn)
    row_grad = home(input_part)
    token_grad = token_sum(mm(own_place, row_grad, tn))
    gate_grad = mm(gate_delta, rows, tn)
    up_grad = mm(up_delta, rows, tn)
    down_grad = mm(hidden, grad_rows, tn)
    return (layer_out, token_grad, gate_grad[None], up_grad[None], down_grad[None])


def solution(mesh):
    in_specs = (
        P("dp", "tensor"),
        P("dp", None),
        P("dp", None),
        P("dp", "expert", "tensor"),
        P("dp", "expert", "tensor"),
        P("dp", "expert", "tensor"),
        P("dp", "tensor"),
    )
    out_specs = (
        P("dp", "tensor"),
        P("dp", "tensor"),
        P("dp", "expert", "tensor"),
        P("dp", "expert", "tensor"),
        P("dp", "expert", "tensor"),
    )
    return jax.shard_map(body, mesh=mesh, in_specs=in_specs, out_specs=out_specs, check_vma=False)
```

profile of v0, /device:TPU:1, one launch (start us, length us, event | category | flops | bytes accessed | tf_op | source)
XLA Modules:
  0.0 376.8 jit_solution(5594621330869188232)
XLA Ops:
  7.2 0.8 fusion.12
  8.0 1.7 reduce-window.6
  9.7 0.3 slice_reduce_fusion
  10.0 0.8 fusion.11
  10.8 0.7 bitcast_add_fusion
  11.6 0.9 select_reduce_fusion
  12.5 1.4 fusion.1
  13.9 0.3 reshape.100
  14.2 45.1 %all_to_all.20 = bf16[16,9,2560]{2,1,0:T(8,128)(2,1)} all-to-all(bf16[16,9,2560]{2,1,0:T(8,128)(2,1)S(1)} %reshape.100), channel_id=1, replica_groups=mesh['dp'=16,'expert'=8,'tensor'=2] {'dp'}, dimensions={0} | all-to-all | bytes 1474560 | tf_op jit(solution)/shard_map/all_to_all | solution.py:35
  59.3 2.5 reshape.101
  61.9 1.4 convolution_convert_fusion.1
  63.3 0.3 reshape.96
  63.6 33.0 %all_to_all.21 = bf16[16,9,2560]{2,1,0:T(8,128)(2,1)} all-to-all(bf16[16,9,2560]{2,1,0:T(8,128)(2,1)S(1)} %reshape.96), channel_id=1, replica_groups=mesh['dp'=16,'expert'=8,'tensor'=2] {'dp'}, dimensions={0} | all-to-all | bytes 1474560 | tf_op jit(solution)/shard_map/all_to_all | solution.py:35
  96.6 2.5 reshape.97
  99.1 2.7 all-gather.5.cloned.1.call-done
  101.9 4.7 %convolution_convert_fusion.4 = bf16[1152,192]{0,1:T(8,128)(2,1)S(1)} fusion(bf16[1152,2560]{1,0:T(8,128)(2,1)} %all-gather.5.cloned.1.call-done, bf16[1,192,2560]{2,1,0:T(8,128)(2,1)S(1)} %copy-done), kind=kOutput, calls=%fused_computation.11 | convolution fusion | flops 1132683264 | bytes 7323648 | tf_op jit(solution)/shard_map/dot_general | solution.py:75
  106.6 5.1 %collective-permute-start.2 = (bf16[1152,192]{0,1:T(8,128)(2,1)S(1)}, bf16[1152,192]{0,1:T(8,128)(2,1)}, u32[]{:S(2)}, u32[]{:S(2)}) collective-permute-start(bf16[1152,192]{0,1:T(8,128)(2,1)S(1)} %convolution_convert_fusion.4), channel_id=1, source_target_pairs={{0,1},{1,0},{2,3},{3,2},{4,5},{5,4},{6,7},{7,6},{8,9},{9,8},{10,11... | collective-permute-start | bytes 1327112 | tf_op jit(solution)/shard_map/ppermute | solution.py:46
  111.7 34.5 %all-gather.3.cloned.1.call-done = bf16[1152,2560]{1,0:T(8,128)(2,1)} async-done(((bf16[144,2560]{1,0:T(8,128)(2,1)}), bf16[1152,2560]{1,0:T(8,128)(2,1)}) %all-gather.3.cloned.1.call-update) | async-done | bytes 5898256 | tf_op jit(solution)/shard_map/all_gather | solution.py:42
  146.2 4.9 %convolution_convert_fusion.6 = bf16[1152,192]{0,1:T(8,128)(2,1)S(1)} fusion(bf16[1152,2560]{1,0:T(8,128)(2,1)} %all-gather.3.cloned.1.call-done, bf16[1,192,2560]{2,1,0:T(8,128)(2,1)S(1)} %copy-done.7), kind=kOutput, calls=%fused_computation.13 | convolution fusion | flops 1132683264 | bytes 7323648 | tf_op jit(solution)/shard_map/dot_general | solution.py:75
  151.1 1.4 collective-permute-start
  152.4 2.1 convolution_convert_fusion.5
  154.5 0.3 collective-permute-start.1
  154.8 7.9 %collective-permute-done = bf16[1152,192]{0,1:T(8,128)(2,1)S(1)} collective-permute-done((bf16[1152,192]{0,1:T(8,128)(2,1)S(1)}, bf16[1152,192]{0,1:T(8,128)(2,1)S(1)}, u32[]{:S(2)}, u32[]{:S(2)}) %collective-permute-start) | collective-permute-done | bytes 442400 | tf_op jit(solution)/shard_map/ppermute | solution.py:46
  162.7 9.5 %collective-permute-done.1 = bf16[1152,192]{0,1:T(8,128)(2,1)S(1)} collective-permute-done((bf16[1152,192]{0,1:T(8,128)(2,1)S(1)}, bf16[1152,192]{0,1:T(8,128)(2,1)S(1)}, u32[]{:S(2)}, u32[]{:S(2)}) %collective-permute-start.1) | collective-permute-done | bytes 442400 | tf_op jit(solution)/shard_map/ppermute | solution.py:46
  172.1 1.8 multiply_convert_fusion
  174.0 4.3 %convolution_convert_fusion = bf16[1152,2560]{1,0:T(8,128)(2,1)} fusion(bf16[1152,192]{0,1:T(8,128)(2,1)S(1)} %get-tuple-element.9, bf16[1,192,2560]{2,1,0:T(8,128)(2,1)S(1)} %copy-done), kind=kOutput, calls=%fused_computation.2 | convolution fusion | flops 1135411200 | bytes 7323648 | tf_op jit(solution)/shard_map/dot_general | solution.py:75
  178.6 0.9 copy-done.8
  179.5 1.7 fusion.6
  181.2 4.3 %fusion = bf16[1152,2560]{1,0:T(8,128)(2,1)} fusion(f32[1152,2560]{1,0:T(8,128)S(1)} %fusion.6, bf16[1152,192]{0,1:T(8,128)(2,1)S(1)} %get-tuple-element.7, bf16[1,192,2560]{2,1,0:T(8,128)(2,1)S(1)} %copy-done.10), kind=kOutput, calls=%fused_computation.1 | convolution fusion | flops 1138360320 | bytes 19120128 | tf_op jit(solution)/shard_map/dot_general | solution.py:75
  185.5 36.0 %reduce-scatter.5.cloned.1.call-done = bf16[144,2560]{1,0:T(8,128)(2,1)} async-done(((bf16[1152,2560]{1,0:T(8,128)(2,1)}), bf16[144,2560]{1,0:T(8,128)(2,1)}) %reduce-scatter.5.cloned.1.call-update) | async-done | bytes 737296 | tf_op jit(solution)/shard_map/reduce_scatter | solution.py:50
  221.5 2.5 reshape.98
  224.0 9.3 %all-to-all-start.1 = ((bf16[16,9,2560]{2,1,0:T(8,128)(2,1)}), bf16[16,9,2560]{2,1,0:T(8,128)(2,1)}, u32[]{:S(2)}, u32[]{:S(2)}) async-start(bf16[16,9,2560]{2,1,0:T(8,128)(2,1)} %reshape.98), calls=%async_computation.2 | async-start | bytes 2621440 | tf_op jit(solution)/shard_map/all_to_all | solution.py:53
  233.3 34.4 %reduce-scatter.9.cloned.1.call-done = bf16[144,2560]{1,0:T(8,128)(2,1)} async-done(((bf16[1152,2560]{1,0:T(8,128)(2,1)}), bf16[144,2560]{1,0:T(8,128)(2,1)}) %reduce-scatter.9.cloned.1.call-update) | async-done | bytes 737296 | tf_op jit(solution)/shard_map/reduce_scatter | solution.py:50
  267.7 2.5 reshape.102
  270.2 9.3 %all-to-all-start.3 = ((bf16[16,9,2560]{2,1,0:T(8,128)(2,1)}), bf16[16,9,2560]{2,1,0:T(8,128)(2,1)S(1)}, u32[]{:S(2)}, u32[]{:S(2)}) async-start(bf16[16,9,2560]{2,1,0:T(8,128)(2,1)} %reshape.102), calls=%async_computation.6 | async-start | bytes 2621440 | tf_op jit(solution)/shard_map/all_to_all | solution.py:53
  279.6 1.6 reshape.99
  281.2 1.2 convolution_convert_fusion.3
  282.5 29.5 %all-to-all-done.3 = bf16[16,9,2560]{2,1,0:T(8,128)(2,1)S(1)} async-done(((bf16[16,9,2560]{2,1,0:T(8,128)(2,1)}), bf16[16,9,2560]{2,1,0:T(8,128)(2,1)S(1)}, u32[]{:S(2)}, u32[]{:S(2)}) %all-to-all-start.3) | async-done | bytes 737312 | tf_op jit(solution)/shard_map/all_to_all | solution.py:53
  312.0 0.3 reshape.103
  312.3 1.2 convolution_convert_fusion.2
  313.6 5.6 %convolution_bitcast_fusion = f32[1,192,2560]{2,1,0:T(8,128)} fusion(bf16[1152,192]{0,1:T(8,128)(2,1)S(1)} %get-tuple-element.9, bf16[1152,2560]{1,0:T(8,128)(2,1)} %all-gather.5.cloned.1.call-done), kind=kOutput, calls=%fused_computation.3 | convolution fusion | flops 1132462080 | bytes 8306688 | tf_op jit(solution)/shard_map/dot_general | solution.py:75
  319.2 2.7 convolution_bitcast_fusion.1
  321.9 2.7 convolution_bitcast_fusion.2
  324.6 17.2 %all_gather.13 = bf16[128,2560]{1,0:T(8,128)(2,1)S(1)} all-gather(bf16[16,2560]{1,0:T(8,128)(2,1)} %reduce-scatter.7.cloned.1.call-done), channel_id=1, replica_groups=mesh['dp'=16,'expert'=8,'tensor'=2] {'expert'}, dimensions={0}, use_global_device_ids=true | all-gather | bytes 737280 | tf_op jit(solution)/shard_map/all_gather | solution.py:66
  341.8 10.3 %reduce-scatter.11.cloned.1.call-done = bf16[16,2560]{1,0:T(8,128)(2,1)} async-done(((bf16[128,2560]{1,0:T(8,128)(2,1)}), bf16[16,2560]{1,0:T(8,128)(2,1)}) %reduce-scatter.11.cloned.1.call-update) | async-done | bytes 81936 | tf_op jit(solution)/shard_map/reduce_scatter | solution.py:63
  352.1 16.1 %all_gather.15 = bf16[128,2560]{1,0:T(8,128)(2,1)S(1)} all-gather(bf16[16,2560]{1,0:T(8,128)(2,1)} %reduce-scatter.11.cloned.1.call-done), channel_id=1, replica_groups=mesh['dp'=16,'expert'=8,'tensor'=2] {'expert'}, dimensions={0}, use_global_device_ids=true | all-gather | bytes 737280 | tf_op jit(solution)/shard_map/all_gather | solution.py:66
  368.3 0.8 copy.18
  369.1 0.8 copy.19
  (46 shorter events, 0.8 us)
Async XLA Ops:
  7.2 94.7 %copy-start = (bf16[1,192,2560]{2,1,0:T(8,128)(2,1)S(1)}, bf16[1,192,2560]{2,1,0:T(8,128)(2,1)}, u32[]{:S(2)}) copy-start(bf16[1,192,2560]{2,1,0:T(8,128)(2,1)} %param.12) | copy-start | bytes 2949124
  7.2 94.7 %all-gather.5.cloned.1.call-start = ((), (), s32[]{:S(2)}) async-start(), calls=%async_computation.11 | async-start | bytes 6635520 | tf_op jit(solution)/shard_map/all_gather | solution.py:42
  61.8 84.4 %all-gather.3.cloned.1.call-start = ((), (), s32[]{:S(2)}) async-start(), calls=%async_computation.8 | async-start | bytes 6635520 | tf_op jit(solution)/shard_map/all_gather | solution.py:42
  99.1 47.1 %copy-start.7 = (bf16[1,192,2560]{2,1,0:T(8,128)(2,1)S(1)}, bf16[1,192,2560]{2,1,0:T(8,128)(2,1)}, u32[]{:S(2)}) copy-start(bf16[1,192,2560]{2,1,0:T(8,128)(2,1)} %param.10) | copy-start | bytes 2949124
  99.1 122.4 %reduce-scatter.5.cloned.1.call-start = ((), (), s32[]{:S(2)}) async-start(), calls=%async_computation.9 | async-start | bytes 6635520 | tf_op jit(solution)/shard_map/reduce_scatter | solution.py:50
  106.6 47.9 %copy-start.11 = (bf16[1152,192]{0,1:T(8,128)(2,1)}, bf16[1152,192]{0,1:T(8,128)(2,1)S(1)}, u32[]{:S(2)}) copy-start(bf16[1152,192]{0,1:T(8,128)(2,1)S(1)} %convolution_convert_fusion.4) | copy-start | bytes 1327108
  106.6 45.8 %copy-start.9 = (bf16[1,192,2560]{2,1,0:T(8,128)(2,1)S(1)}, bf16[1,192,2560]{2,1,0:T(8,128)(2,1)}, u32[]{:S(2)}) copy-start(bf16[1,192,2560]{2,1,0:T(8,128)(2,1)} %param.11) | copy-start | bytes 2949124
  106.6 48.2 %collective-permute-start.2 = (bf16[1152,192]{0,1:T(8,128)(2,1)S(1)}, bf16[1152,192]{0,1:T(8,128)(2,1)}, u32[]{:S(2)}, u32[]{:S(2)}) collective-permute-start(bf16[1152,192]{0,1:T(8,128)(2,1)S(1)} %convolution_convert_fusion.4), channel_id=1, source_target_pairs={{0,1},{1,0},{2,3},{3,2},{4,5},{5,4},{6,7},{7,6},{8,9},{9,8},{10,11... | collective-permute-start | bytes 1327112 | tf_op jit(solution)/shard_map/ppermute | solution.py:46
  146.2 6.3 %copy-start.2 = (bf16[1152,2560]{1,0:T(8,128)(2,1)S(1)}, bf16[1152,2560]{1,0:T(8,128)(2,1)}, u32[]{:S(2)}) copy-start(bf16[1152,2560]{1,0:T(8,128)(2,1)} %all-gather.3.cloned.1.call-done) | copy-start | bytes 17694724
  151.1 11.6 %collective-permute-start = (bf16[1152,192]{0,1:T(8,128)(2,1)S(1)}, bf16[1152,192]{0,1:T(8,128)(2,1)S(1)}, u32[]{:S(2)}, u32[]{:S(2)}) collective-permute-start(bf16[1152,192]{0,1:T(8,128)(2,1)S(1)} %convolution_convert_fusion.6), channel_id=1, source_target_pairs={{0,1},{1,0},{2,3},{3,2},{4,5},{5,4},{6,7},{7,6},{8,9},{9,8},{10,11... | collective-permute-start | bytes 1327112 | tf_op jit(solution)/shard_map/ppermute | solution.py:46
  154.5 17.6 %collective-permute-start.1 = (bf16[1152,192]{0,1:T(8,128)(2,1)S(1)}, bf16[1152,192]{0,1:T(8,128)(2,1)S(1)}, u32[]{:S(2)}, u32[]{:S(2)}) collective-permute-start(bf16[1152,192]{0,1:T(8,128)(2,1)S(1)} %convolution_convert_fusion.5), channel_id=1, source_target_pairs={{0,1},{1,0},{2,3},{3,2},{4,5},{5,4},{6,7},{7,6},{8,9},{9,8},{10,11... | collective-permute-start | bytes 1327112 | tf_op jit(solution)/shard_map/ppermute | solution.py:46
  174.0 4.6 %copy-start.3 = (bf16[1152,192]{0,1:T(8,128)(2,1)}, bf16[1152,192]{0,1:T(8,128)(2,1)S(1)}, u32[]{:S(2)}) copy-start(bf16[1152,192]{0,1:T(8,128)(2,1)S(1)} %get-tuple-element.8) | copy-start | bytes 1327108
  174.0 7.2 %copy-start.5 = (bf16[1152,192]{0,1:T(8,128)(2,1)}, bf16[1152,192]{0,1:T(8,128)(2,1)S(1)}, u32[]{:S(2)}) copy-start(bf16[1152,192]{0,1:T(8,128)(2,1)S(1)} %get-tuple-element.7) | copy-start | bytes 1327108
  178.3 1.2 copy-start.8
  178.3 89.4 %reduce-scatter.9.cloned.1.call-start = ((), (), s32[]{:S(2)}) async-start(), calls=%async_computation.12 | async-start | bytes 6635520 | tf_op jit(solution)/shard_map/reduce_scatter | solution.py:50
  179.5 1.8 copy-start.10
  224.0 46.2 %all-to-all-start.1 = ((bf16[16,9,2560]{2,1,0:T(8,128)(2,1)}), bf16[16,9,2560]{2,1,0:T(8,128)(2,1)}, u32[]{:S(2)}, u32[]{:S(2)}) async-start(bf16[16,9,2560]{2,1,0:T(8,128)(2,1)} %reshape.98), calls=%async_computation.2 | async-start | bytes 2621440 | tf_op jit(solution)/shard_map/all_to_all | solution.py:53
  270.2 41.8 %all-to-all-start.3 = ((bf16[16,9,2560]{2,1,0:T(8,128)(2,1)}), bf16[16,9,2560]{2,1,0:T(8,128)(2,1)S(1)}, u32[]{:S(2)}, u32[]{:S(2)}) async-start(bf16[16,9,2560]{2,1,0:T(8,128)(2,1)} %reshape.102), calls=%async_computation.6 | async-start | bytes 2621440 | tf_op jit(solution)/shard_map/all_to_all | solution.py:53
  279.5 45.1 %reduce-scatter.7.cloned.1.call-start = ((), (), s32[]{:S(2)}) async-start(), calls=%async_computation.10 | async-start | bytes 737280 | tf_op jit(solution)/shard_map/reduce_scatter | solution.py:63
  282.4 69.7 %reduce-scatter.11.cloned.1.call-start = ((), (), s32[]{:S(2)}) async-start(), calls=%async_computation.13 | async-start | bytes 737280 | tf_op jit(solution)/shard_map/reduce_scatter | solution.py:63
  312.3 6.8 %slice-start = ((s8[5898240]{0:T(1024)(128)(4,1)}), s8[1703936]{0:T(1024)(128)(4,1)S(1)}, s32[]{:S(2)}) async-start(s8[5898240]{0:T(1024)(128)(4,1)} %bitcast.64), calls=%async_computation.14 | async-start | bytes 3407872
  313.6 5.6 %slice-start.1 = ((s8[5898240]{0:T(1024)(128)(4,1)}), s8[4194304]{0:T(1024)(128)(4,1)S(1)}, s32[]{:S(2)}) async-start(s8[5898240]{0:T(1024)(128)(4,1)} %bitcast.64), calls=%async_computation.15 | async-start | bytes 8388608
  313.6 5.6 %copy-start.6 = (bf16[1152,192]{0,1:T(8,128)(2,1)S(1)}, bf16[1152,192]{0,1:T(8,128)(2,1)}, u32[]{:S(2)}) copy-start(bf16[1152,192]{0,1:T(8,128)(2,1)} %copy-done.5) | copy-start | bytes 1327108
  319.2 2.7 copy-start.4
  319.2 50.8 %copy-start.1 = (bf16[1,192,2560]{2,1,0:T(8,128)(2,1)S(1)}, bf16[1,192,2560]{2,1,0:T(8,128)(2,1)}, u32[]{:S(2)}) copy-start(bf16[1,192,2560]{2,1,0:T(8,128)(2,1)} %param.12) | copy-start | bytes 2949124
Sparse Core Ops, SparseCore 0:
  61.9 39.8 all-gather.4
  104.3 41.8 all-gather.2
  178.4 43.0 reduce-scatter.4
  224.1 43.5 reduce-scatter.8
  283.2 33.1 reduce-scatter.6
  319.3 32.7 reduce-scatter.10
where the time goes:
time: 378 us; the launch traced here: 377 us
  waiting for transfers between devices  165 us (44%)
  blocking collectives  111 us (29%)
  matrix products  38.2 us (10%)
  starting transfers between devices  25.7 us (7%)
  local copies, waits for them, and re-layouts  15.4 us (4%)
  between operations  14.4 us (4%)
  other arithmetic  6.83 us (2%)
    all_to_all x2, blocking collectives, dispatch(): lax.all_to_all(rows.reshape(dp_count, share_rows, half_width), 'dp', spli...  78 us
    reduce_scatter x2, waiting for transfers between devices, home(): lax.psum_scatter(partial_rows.astype(jnp.bfloat16), 'expert', scatter_dim...  70.4 us
    all_gather x2, waiting for transfers between devices, dispatch(): lax.all_gather(arrived.reshape(own_rows, half_width), 'expert', axis=0, t...  37.2 us
    dot_general x11, matrix products, mm(): return lax.dot_general(a, b, dims, preferred_element_type=jnp.float32)  35.3 us
    all_gather x2, blocking collectives, token_sum(): return lax.all_gather(part, 'expert', axis=0, tiled=True)  33.3 us
    all_to_all x2, waiting for transfers between devices, home(): lax.all_to_all(summed.reshape(dp_count, share_rows, half_width), 'dp', sp...  29.5 us
    all_to_all x2, starting transfers between devices, home(): lax.all_to_all(summed.reshape(dp_count, share_rows, half_width), 'dp', sp...  18.6 us
    ppermute x3, waiting for transfers between devices, width_sum(): other = lax.ppermute(mine, 'tensor', [(0, 1), (1, 0)])  17.4 us
  transfers between devices with their start and end apart: 11, of which 8 were waited for; matrix products, arithmetic and copies ran while one was open for 11% of the time, Pallas kernels for 0%

commit v1 on v0

--- a/solution.py
+++ b/solution.py
@@ -39,7 +39,15 @@
             concat_axis=0,
             tiled=True,
         )
-        return lax.all_gather(arrived.reshape(own_rows, half_width), "expert", axis=0, tiled=True)
+        return jnp.concatenate(
+            lax.all_to_all(
+                jnp.stack([arrived.reshape(own_rows, half_width)] * lax.axis_size("expert")),
+                "expert",
+                0,
+                0,
+            ),
+            axis=0,
+        )
 
     def width_sum(partial_values):
         mine = partial_values.astype(jnp.bfloat16)

time: 378 us -> 468 us (1.24)
  waiting for transfers between devices: 165 us -> 284 us
  blocking collectives: 111 us -> 33.9 us
  starting transfers between devices: 25.7 us -> 59.4 us
  matrix products: 38.2 us -> 47.6 us
  local copies, waits for them, and re-layouts: 15.4 us -> 21.7 us
    all_to_all x0 -> x4, waiting for transfers between devices: none -> 176 us  [the longest x2 120 us: dispatch(): lax.all_to_all(jnp.stack([arrived.reshape(own_rows, half_width)] * lax.ax...]
    all_to_all x2 -> x0, blocking collectives: 78 us -> none  [dispatch(): lax.all_to_all(rows.reshape(dp_count, share_rows, half_width), 'dp', spli...]
    all_to_all x0 -> x4, starting transfers between devices: none -> 38.9 us  [the longest x2 19.6 us: dispatch(): lax.all_to_all(rows.reshape(dp_count, share_rows, half_width), 'dp', spli...]
    all_gather x2 -> x0, waiting for transfers between devices: 37.2 us -> none  [dispatch(): lax.all_gather(arrived.reshape(own_rows, half_width), 'expert', axis=0, t...]
    dot_general x11, matrix products: 35.3 us -> 44.8 us  [mm(): return lax.dot_general(a, b, dims, preferred_element_type=jnp.float32)]
    another operation x0 -> x4, local copies, waits for them, and re-layouts: none -> 8.05 us  [dispatch(): jnp.stack([arrived.reshape(own_rows, half_width)] * lax.axis_size('expert'))]
    ppermute x3, waiting for transfers between devices: 17.4 us -> 10 us  [width_sum(): other = lax.ppermute(mine, 'tensor', [(0, 1), (1, 0)])]
    reduce_scatter x2, waiting for transfers between devices: 10.3 us -> 4.09 us  [token_sum(): lax.psum_scatter(partial_tokens.astype(jnp.bfloat16), 'expert', scatter_d...]
  transfers between devices with their start and end apart: 11 -> 13, of which waited for: 8 -> 9; matrix products, arithmetic and copies ran while one was open for 11% -> 11% of each run, Pallas kernels for 0% -> 0%
where the time goes in v1:
time: 468 us; the launch traced here: 467 us
  waiting for transfers between devices  284 us (61%)
  starting transfers between devices  59.4 us (13%)
  matrix products  47.6 us (10%)
  blocking collectives  33.9 us (7%)
  local copies, waits for them, and re-layouts  21.7 us (5%)
  between operations  13.9 us (3%)
  other arithmetic  6.41 us (1%)
    all_to_all x2, waiting for transfers between devices, dispatch(): lax.all_to_all(jnp.stack([arrived.reshape(own_rows, half_width)] * lax.ax...  120 us
    reduce_scatter x2, waiting for transfers between devices, home(): lax.psum_scatter(partial_rows.astype(jnp.bfloat16), 'expert', scatter_dim...  64.7 us
    all_to_all x2, waiting for transfers between devices, dispatch(): lax.all_to_all(rows.reshape(dp_count, share_rows, half_width), 'dp', spli...  55.8 us
    dot_general x11, matrix products, mm(): return lax.dot_general(a, b, dims, preferred_element_type=jnp.float32)  44.8 us
    all_gather x2, blocking collectives, token_sum(): return lax.all_gather(part, 'expert', axis=0, tiled=True)  33.9 us
    all_to_all x2, waiting for transfers between devices, home(): lax.all_to_all(summed.reshape(dp_count, share_rows, half_width), 'dp', sp...  29.5 us
    all_to_all x2, starting transfers between devices, dispatch(): lax.all_to_all(rows.reshape(dp_count, share_rows, half_width), 'dp', spli...  19.6 us
    all_to_all x2, starting transfers between devices, dispatch(): lax.all_to_all(jnp.stack([arrived.reshape(own_rows, half_width)] * lax.ax...  19.2 us
  transfers between devices with their start and end apart: 13, of which 9 were waited for; matrix products, arithmetic and copies ran while one was open for 11% of the time, Pallas kernels for 0%

profile of v1, /device:TPU:1, one launch (start us, length us, event | category | flops | bytes accessed | tf_op | source)
XLA Modules:
  0.0 467.2 jit_solution(15004446328463177612)
XLA Ops:
  7.2 0.8 fusion.12
  8.0 1.7 reduce-window.6
  10.0 0.8 fusion.11
  10.7 0.7 bitcast_add_fusion
  11.6 1.4 convolution_convert_fusion.1
  13.0 1.4 reshape.100
  14.4 11.7 %all-to-all-start = ((bf16[16,9,2560]{2,1,0:T(8,128)(2,1)}), bf16[16,9,2560]{2,1,0:T(8,128)(2,1)S(1)}, u32[]{:S(2)}, u32[]{:S(2)}) async-start(bf16[16,9,2560]{2,1,0:T(8,128)(2,1)} %reshape.100), calls=%async_computation | async-start | bytes 2621440 | tf_op jit(solution)/shard_map/all_to_all | solution.py:35
  26.3 1.4 fusion.1
  27.8 1.4 reshape.104
  29.1 27.5 %all-to-all-done = bf16[16,9,2560]{2,1,0:T(8,128)(2,1)S(1)} async-done(((bf16[16,9,2560]{2,1,0:T(8,128)(2,1)}), bf16[16,9,2560]{2,1,0:T(8,128)(2,1)S(1)}, u32[]{:S(2)}, u32[]{:S(2)}) %all-to-all-start) | async-done | bytes 737312 | tf_op jit(solution)/shard_map/all_to_all | solution.py:35
  56.6 7.9 %all-to-all-start.3 = ((bf16[16,9,2560]{2,1,0:T(8,128)(2,1)}), bf16[16,9,2560]{2,1,0:T(8,128)(2,1)}, u32[]{:S(2)}, u32[]{:S(2)}) async-start(bf16[16,9,2560]{2,1,0:T(8,128)(2,1)} %reshape.104), calls=%async_computation.5 | async-start | bytes 2621440 | tf_op jit(solution)/shard_map/all_to_all | solution.py:35
  64.8 28.3 %all-to-all-done.3 = bf16[16,9,2560]{2,1,0:T(8,128)(2,1)} async-done(((bf16[16,9,2560]{2,1,0:T(8,128)(2,1)}), bf16[16,9,2560]{2,1,0:T(8,128)(2,1)}, u32[]{:S(2)}, u32[]{:S(2)}) %all-to-all-start.3) | async-done | bytes 737312 | tf_op jit(solution)/shard_map/all_to_all | solution.py:35
  93.1 3.1 stack.6
  96.2 13.6 %all-to-all-start.1 = ((bf16[8,144,2560]{2,1,0:T(8,128)(2,1)}), bf16[8,144,2560]{2,1,0:T(8,128)(2,1)}, u32[]{:S(2)}, u32[]{:S(2)}) async-start(bf16[8,144,2560]{2,1,0:T(8,128)(2,1)} %stack.6), calls=%async_computation.1 | async-start | bytes 11796480 | tf_op jit(solution)/shard_map/all_to_all | solution.py:43
  109.8 1.6 stack_reshape.5
  111.5 65.6 %all-to-all-done.1 = bf16[8,144,2560]{2,1,0:T(8,128)(2,1)} async-done(((bf16[8,144,2560]{2,1,0:T(8,128)(2,1)}), bf16[8,144,2560]{2,1,0:T(8,128)(2,1)}, u32[]{:S(2)}, u32[]{:S(2)}) %all-to-all-start.1) | async-done | bytes 5898272 | tf_op jit(solution)/shard_map/all_to_all | solution.py:43
  177.0 3.0 stack.7
  180.1 5.6 %all-to-all-start.4 = ((bf16[8,144,2560]{2,1,0:T(8,128)(2,1)}), bf16[8,144,2560]{2,1,0:T(8,128)(2,1)}, u32[]{:S(2)}, u32[]{:S(2)}) async-start(bf16[8,144,2560]{2,1,0:T(8,128)(2,1)} %stack.7), calls=%async_computation.6 | async-start | bytes 11796480 | tf_op jit(solution)/shard_map/all_to_all | solution.py:43
  185.7 5.6 %convolution_convert_fusion.6 = bf16[1152,192]{0,1:T(8,128)(2,1)} fusion(bf16[1152,2560]{1,0:T(8,128)(2,1)} %bitcast.5, bf16[1,192,2560]{2,1,0:T(8,128)(2,1)S(1)} %copy-done.2), kind=kOutput, calls=%fused_computation.13 | convolution fusion | flops 1132683264 | bytes 7323648 | tf_op jit(solution)/shard_map/dot_general | solution.py:83
  191.2 5.5 %convolution_convert_fusion.5 = bf16[1152,192]{0,1:T(8,128)(2,1)} fusion(bf16[1152,2560]{1,0:T(8,128)(2,1)} %bitcast.5, bf16[1,192,2560]{2,1,0:T(8,128)(2,1)S(1)} %copy-done.3), kind=kOutput, calls=%fused_computation.12 | convolution fusion | flops 1132683264 | bytes 7323648 | tf_op jit(solution)/shard_map/dot_general | solution.py:83
  196.7 1.5 collective-permute-start.1
  198.2 54.6 %all-to-all-done.4 = bf16[8,144,2560]{2,1,0:T(8,128)(2,1)} async-done(((bf16[8,144,2560]{2,1,0:T(8,128)(2,1)}), bf16[8,144,2560]{2,1,0:T(8,128)(2,1)}, u32[]{:S(2)}, u32[]{:S(2)}) %all-to-all-start.4) | async-done | bytes 5898272 | tf_op jit(solution)/shard_map/all_to_all | solution.py:43
  252.8 4.7 %convolution_convert_fusion.4 = bf16[1152,192]{0,1:T(8,128)(2,1)S(1)} fusion(bf16[1152,2560]{1,0:T(8,128)(2,1)} %bitcast.9, bf16[1,192,2560]{2,1,0:T(8,128)(2,1)S(1)} %copy-done), kind=kOutput, calls=%fused_computation.11 | convolution fusion | flops 1132683264 | bytes 7323648 | tf_op jit(solution)/shard_map/dot_general | solution.py:83
  257.7 0.8 copy-done.5
  258.5 10.0 %collective-permute-done.2 = bf16[1152,192]{0,1:T(8,128)(2,1)S(1)} collective-permute-done((bf16[1152,192]{0,1:T(8,128)(2,1)S(1)}, bf16[1152,192]{0,1:T(8,128)(2,1)S(1)}, u32[]{:S(2)}, u32[]{:S(2)}) %collective-permute-start.2) | collective-permute-done | bytes 442400 | tf_op jit(solution)/shard_map/ppermute | solution.py:54
  268.5 2.1 multiply_convert_fusion
  270.6 4.3 convolution_convert_fusion
  275.1 1.7 fusion.6
  276.9 4.3 fusion
  281.1 30.0 %reduce-scatter.5.cloned.1.call-done = bf16[144,2560]{1,0:T(8,128)(2,1)} async-done(((bf16[1152,2560]{1,0:T(8,128)(2,1)}), bf16[144,2560]{1,0:T(8,128)(2,1)}) %reduce-scatter.5.cloned.1.call-update) | async-done | bytes 737296 | tf_op jit(solution)/shard_map/reduce_scatter | solution.py:58
  311.2 2.5 reshape.102
  313.6 9.3 %all-to-all-start.2 = ((bf16[16,9,2560]{2,1,0:T(8,128)(2,1)}), bf16[16,9,2560]{2,1,0:T(8,128)(2,1)}, u32[]{:S(2)}, u32[]{:S(2)}) async-start(bf16[16,9,2560]{2,1,0:T(8,128)(2,1)} %reshape.102), calls=%async_computation.3 | async-start | bytes 2621440 | tf_op jit(solution)/shard_map/all_to_all | solution.py:61
  323.0 34.7 %reduce-scatter.9.cloned.1.call-done = bf16[144,2560]{1,0:T(8,128)(2,1)} async-done(((bf16[1152,2560]{1,0:T(8,128)(2,1)}), bf16[144,2560]{1,0:T(8,128)(2,1)}) %reduce-scatter.9.cloned.1.call-update) | async-done | bytes 737296 | tf_op jit(solution)/shard_map/reduce_scatter | solution.py:58
  357.6 2.5 reshape.106
  360.1 9.3 %all-to-all-start.5 = ((bf16[16,9,2560]{2,1,0:T(8,128)(2,1)}), bf16[16,9,2560]{2,1,0:T(8,128)(2,1)}, u32[]{:S(2)}, u32[]{:S(2)}) async-start(bf16[16,9,2560]{2,1,0:T(8,128)(2,1)} %reshape.106), calls=%async_computation.8 | async-start | bytes 2621440 | tf_op jit(solution)/shard_map/all_to_all | solution.py:61
  369.5 1.6 reshape.103
  371.1 1.2 convolution_convert_fusion.3
  372.4 29.5 %all-to-all-done.5 = bf16[16,9,2560]{2,1,0:T(8,128)(2,1)} async-done(((bf16[16,9,2560]{2,1,0:T(8,128)(2,1)}), bf16[16,9,2560]{2,1,0:T(8,128)(2,1)}, u32[]{:S(2)}, u32[]{:S(2)}) %all-to-all-start.5) | async-done | bytes 737312 | tf_op jit(solution)/shard_map/all_to_all | solution.py:61
  401.9 1.6 reshape.107
  403.5 1.2 convolution_convert_fusion.2
  404.8 5.4 %convolution_bitcast_fusion = f32[1,192,2560]{2,1,0:T(8,128)} fusion(bf16[1152,192]{0,1:T(8,128)(2,1)S(1)} %get-tuple-element.9, bf16[1152,2560]{1,0:T(8,128)(2,1)} %bitcast.9), kind=kOutput, calls=%fused_computation.3 | convolution fusion | flops 1132462080 | bytes 8306688 | tf_op jit(solution)/shard_map/dot_general | solution.py:83
  410.2 5.5 %convolution_bitcast_fusion.1 = f32[1,192,2560]{2,1,0:T(8,128)} fusion(bf16[1152,192]{0,1:T(8,128)(2,1)S(1)} %get-tuple-element.7, bf16[1152,2560]{1,0:T(8,128)(2,1)} %bitcast.5), kind=kOutput, calls=%fused_computation.4 | convolution fusion | flops 1132462080 | bytes 8306688 | tf_op jit(solution)/shard_map/dot_general | solution.py:83
  415.7 5.4 %convolution_bitcast_fusion.2 = f32[1,192,2560]{2,1,0:T(8,128)} fusion(bf16[1152,192]{0,1:T(8,128)(2,1)S(1)} %get-tuple-element.8, bf16[1152,2560]{1,0:T(8,128)(2,1)} %bitcast.5), kind=kOutput, calls=%fused_computation.5 | convolution fusion | flops 1132462080 | bytes 8306688 | tf_op jit(solution)/shard_map/dot_general | solution.py:83
  421.1 17.3 %all_gather.6 = bf16[128,2560]{1,0:T(8,128)(2,1)S(1)} all-gather(bf16[16,2560]{1,0:T(8,128)(2,1)} %reduce-scatter.7.cloned.1.call-done), channel_id=1, replica_groups=mesh['dp'=16,'expert'=8,'tensor'=2] {'expert'}, dimensions={0}, use_global_device_ids=true | all-gather | bytes 737280 | tf_op jit(solution)/shard_map/all_gather | solution.py:74
  438.4 4.1 reduce-scatter.11.cloned.1.call-done
  442.5 16.5 %all_gather.7 = bf16[128,2560]{1,0:T(8,128)(2,1)S(1)} all-gather(bf16[16,2560]{1,0:T(8,128)(2,1)} %reduce-scatter.11.cloned.1.call-done), channel_id=1, replica_groups=mesh['dp'=16,'expert'=8,'tensor'=2] {'expert'}, dimensions={0}, use_global_device_ids=true | all-gather | bytes 737280 | tf_op jit(solution)/shard_map/all_gather | solution.py:74
  459.0 0.8 copy.18
  459.9 0.8 copy.19
  (33 shorter events, 1.4 us)
Async XLA Ops:
  7.2 245.7 %copy-start = (bf16[1,192,2560]{2,1,0:T(8,128)(2,1)S(1)}, bf16[1,192,2560]{2,1,0:T(8,128)(2,1)}, u32[]{:S(2)}) copy-start(bf16[1,192,2560]{2,1,0:T(8,128)(2,1)} %param.12) | copy-start | bytes 2949124
  7.2 18.9 %copy-start.6 = (f32[128,6]{0,1:T(8,128)S(1)}, f32[128,6]{0,1:T(8,128)}, u32[]{:S(2)}) copy-start(f32[128,6]{0,1:T(8,128)} %param.9) | copy-start | bytes 9220
  14.4 42.3 %all-to-all-start = ((bf16[16,9,2560]{2,1,0:T(8,128)(2,1)}), bf16[16,9,2560]{2,1,0:T(8,128)(2,1)S(1)}, u32[]{:S(2)}, u32[]{:S(2)}) async-start(bf16[16,9,2560]{2,1,0:T(8,128)(2,1)} %reshape.100), calls=%async_computation | async-start | bytes 2621440 | tf_op jit(solution)/shard_map/all_to_all | solution.py:35
  56.6 36.5 %all-to-all-start.3 = ((bf16[16,9,2560]{2,1,0:T(8,128)(2,1)}), bf16[16,9,2560]{2,1,0:T(8,128)(2,1)}, u32[]{:S(2)}, u32[]{:S(2)}) async-start(bf16[16,9,2560]{2,1,0:T(8,128)(2,1)} %reshape.104), calls=%async_computation.5 | async-start | bytes 2621440 | tf_op jit(solution)/shard_map/all_to_all | solution.py:35
  96.2 80.8 %all-to-all-start.1 = ((bf16[8,144,2560]{2,1,0:T(8,128)(2,1)}), bf16[8,144,2560]{2,1,0:T(8,128)(2,1)}, u32[]{:S(2)}, u32[]{:S(2)}) async-start(bf16[8,144,2560]{2,1,0:T(8,128)(2,1)} %stack.6), calls=%async_computation.1 | async-start | bytes 11796480 | tf_op jit(solution)/shard_map/all_to_all | solution.py:43
  180.0 5.6 %copy-start.2 = (bf16[1,192,2560]{2,1,0:T(8,128)(2,1)S(1)}, bf16[1,192,2560]{2,1,0:T(8,128)(2,1)}, u32[]{:S(2)}) copy-start(bf16[1,192,2560]{2,1,0:T(8,128)(2,1)} %param.10) | copy-start | bytes 2949124
  180.1 72.8 %all-to-all-start.4 = ((bf16[8,144,2560]{2,1,0:T(8,128)(2,1)}), bf16[8,144,2560]{2,1,0:T(8,128)(2,1)}, u32[]{:S(2)}, u32[]{:S(2)}) async-start(bf16[8,144,2560]{2,1,0:T(8,128)(2,1)} %stack.7), calls=%async_computation.6 | async-start | bytes 11796480 | tf_op jit(solution)/shard_map/all_to_all | solution.py:43
  185.6 5.6 %copy-start.3 = (bf16[1,192,2560]{2,1,0:T(8,128)(2,1)S(1)}, bf16[1,192,2560]{2,1,0:T(8,128)(2,1)}, u32[]{:S(2)}) copy-start(bf16[1,192,2560]{2,1,0:T(8,128)(2,1)} %param.11) | copy-start | bytes 2949124
  185.7 125.5 %reduce-scatter.5.cloned.1.call-start = ((), (), s32[]{:S(2)}) async-start(), calls=%async_computation.10 | async-start | bytes 6635520 | tf_op jit(solution)/shard_map/reduce_scatter | solution.py:58
  191.2 66.4 %collective-permute-start = (bf16[1152,192]{0,1:T(8,128)(2,1)}, bf16[1152,192]{0,1:T(8,128)(2,1)}, u32[]{:S(2)}, u32[]{:S(2)}) collective-permute-start(bf16[1152,192]{0,1:T(8,128)(2,1)} %convolution_convert_fusion.6), channel_id=1, source_target_pairs={{0,1},{1,0},{2,3},{3,2},{4,5},{5,4},{6,7},{7,6},{8,9},{9,8},{10,11... | collective-permute-start | bytes 1327112 | tf_op jit(solution)/shard_map/ppermute | solution.py:54
  196.7 60.9 %collective-permute-start.1 = (bf16[1152,192]{0,1:T(8,128)(2,1)}, bf16[1152,192]{0,1:T(8,128)(2,1)S(1)}, u32[]{:S(2)}, u32[]{:S(2)}) collective-permute-start(bf16[1152,192]{0,1:T(8,128)(2,1)} %convolution_convert_fusion.5), channel_id=1, source_target_pairs={{0,1},{1,0},{2,3},{3,2},{4,5},{5,4},{6,7},{7,6},{8,9},{9,8},{10,11... | collective-permute-start | bytes 1327112 | tf_op jit(solution)/shard_map/ppermute | solution.py:54
  257.6 10.9 %collective-permute-start.2 = (bf16[1152,192]{0,1:T(8,128)(2,1)S(1)}, bf16[1152,192]{0,1:T(8,128)(2,1)S(1)}, u32[]{:S(2)}, u32[]{:S(2)}) collective-permute-start(bf16[1152,192]{0,1:T(8,128)(2,1)S(1)} %convolution_convert_fusion.4), channel_id=1, source_target_pairs={{0,1},{1,0},{2,3},{3,2},{4,5},{5,4},{6,7},{7,6},{8,9},{9,8},{10,11... | collective-permute-start | bytes 1327112 | tf_op jit(solution)/shard_map/ppermute | solution.py:54
  257.7 0.8 copy-start.5
  274.9 82.7 %reduce-scatter.9.cloned.1.call-start = ((), (), s32[]{:S(2)}) async-start(), calls=%async_computation.12 | async-start | bytes 6635520 | tf_op jit(solution)/shard_map/reduce_scatter | solution.py:58
  275.1 1.8 copy-start.4
  313.6 46.4 %all-to-all-start.2 = ((bf16[16,9,2560]{2,1,0:T(8,128)(2,1)}), bf16[16,9,2560]{2,1,0:T(8,128)(2,1)}, u32[]{:S(2)}, u32[]{:S(2)}) async-start(bf16[16,9,2560]{2,1,0:T(8,128)(2,1)} %reshape.102), calls=%async_computation.3 | async-start | bytes 2621440 | tf_op jit(solution)/shard_map/all_to_all | solution.py:61
  360.1 41.8 %all-to-all-start.5 = ((bf16[16,9,2560]{2,1,0:T(8,128)(2,1)}), bf16[16,9,2560]{2,1,0:T(8,128)(2,1)}, u32[]{:S(2)}, u32[]{:S(2)}) async-start(bf16[16,9,2560]{2,1,0:T(8,128)(2,1)} %reshape.106), calls=%async_computation.8 | async-start | bytes 2621440 | tf_op jit(solution)/shard_map/all_to_all | solution.py:61
  369.4 51.6 %reduce-scatter.7.cloned.1.call-start = ((), (), s32[]{:S(2)}) async-start(), calls=%async_computation.11 | async-start | bytes 737280 | tf_op jit(solution)/shard_map/reduce_scatter | solution.py:71
  372.4 70.1 %reduce-scatter.11.cloned.1.call-start = ((), (), s32[]{:S(2)}) async-start(), calls=%async_computation.13 | async-start | bytes 737280 | tf_op jit(solution)/shard_map/reduce_scatter | solution.py:71
  410.2 50.5 %copy-start.1 = (bf16[1,192,2560]{2,1,0:T(8,128)(2,1)S(1)}, bf16[1,192,2560]{2,1,0:T(8,128)(2,1)}, u32[]{:S(2)}) copy-start(bf16[1,192,2560]{2,1,0:T(8,128)(2,1)} %param.12) | copy-start | bytes 2949124
Sparse Core Ops, SparseCore 0:
  275.0 36.1 reduce-scatter.4
  313.9 43.6 reduce-scatter.8
  373.4 33.4 reduce-scatter.6
  409.9 32.5 reduce-scatter.10
